TPU v7x, 256 devices: a whole 4x4x8 slice. The times are simulated.
256 devices in a mesh: grp: 16 (over z_lo, x, core), peak: 16 (over y, z_hi).
Axes of the slice: x: 4, y: 4, z: 8 (z_hi: 4, z_lo: 2; z = z_hi * 2 + z_lo), core: 2. Of those that a mesh axis runs over, the one named last changes fastest.
Arguments:
- counts: bfloat16 [1024, 524288], P(None, ('grp', 'peak')), may hold values from 0.099609375 to 4
- tile_mask: int32 [1024, 4096], P(None, ('grp', 'peak')), may hold values 0 or 1
- neighbours: int32 [1024, 15], P(('grp', 'peak')), may hold values from 0 to 1023, as said below
- peak_weight: bfloat16 [524288, 512], P(('grp', 'peak')), may hold values from -0.013671875 to 0.013671875
- gain: float32 [512], replicated, may hold values from 0.25 to 1.75
- w_in: bfloat16 [512, 512], replicated, may hold values from -0.25 to 0.25
- w_out: bfloat16 [512, 256], replicated, may hold values from -0.25 to 0.25
Outputs:
- peak_grad: float32 [524288, 512], P(('grp', 'peak'))
- gain_grad: float32 [512], replicated
- in_grad: float32 [512, 512], replicated
- out_grad: float32 [512, 256], replicated
Inputs may be any that keep to these rules, and one draw needn't show every extreme that they name: `neighbours`: every entry is a cell index other than its own row's cell.
All inputs are finite; a program needn't handle non-finite values. No bound on the sum of `tile_mask` on one device may be relied on, other than what follows from the above.
Results may differ from a plain program's by a relative error of at most 0.012.
Values may be sent and summed in bfloat16 or wider, within the bound.
A program may use at most 64 MiB of HBM per device.

v0:
```python
import jax
import jax.numpy as jnp
from jax import lax
from jax.sharding import PartitionSpec as P

TILE = 128
K = 15
sharpness_divisor = 0.2
eps_norm = 1e-06
gelu_coef = 0.7978845608
cubic_coef = 0.044715


def gelu_tanh(values):
    return (
        0.5
        * values
        * (1.0 + jnp.tanh(gelu_coef * (values + cubic_coef * values * values * values)))
    )


def gelu_slope(values):
    tangent = jnp.tanh(gelu_coef * (values + cubic_coef * values * values * values))
    return 0.5 * (1.0 + tangent) + 0.5 * values * (1.0 - tangent * tangent) * gelu_coef * (
        1.0 + 3.0 * cubic_coef * values * values
    )


def collapsed_lines(left, right):
    return lax.dot_general(
        left, right, (((0,), (0,)), ((), ())), preferred_element_type=jnp.float32
    )


def tower_forward(hidden, gain, w_in, w_out):
    scale = lax.rsqrt(jnp.mean(hidden * hidden, axis=1, keepdims=True) + eps_norm)
    normed = hidden * scale
    rounded = (normed * gain[None, :]).astype(jnp.bfloat16)
    preact = jnp.dot(rounded, w_in, preferred_element_type=jnp.float32)
    activ = gelu_tanh(preact).astype(jnp.bfloat16)
    project = jnp.dot(activ, w_out, preferred_element_type=jnp.float32)
    length = lax.rsqrt(jnp.sum(project * project, axis=1, keepdims=True) + eps_norm)
    unit = project * length
    return ((scale, normed, rounded, preact, activ, length, unit), unit.astype(jnp.bfloat16))


def tower_backward(vector_derivative, gain, w_in, w_out, saved):
    scale, normed, rounded, preact, activ, length, unit = saved
    dproj = (
        length
        * (vector_derivative - unit * jnp.sum(unit * vector_derivative, axis=1, keepdims=True))
    ).astype(jnp.bfloat16)
    out_grad = collapsed_lines(activ, dproj)
    dact = jnp.dot(dproj, w_out.T, preferred_element_type=jnp.float32)
    dpre = (dact * gelu_slope(preact)).astype(jnp.bfloat16)
    in_grad = collapsed_lines(rounded, dpre)
    dround = jnp.dot(dpre, w_in.T, preferred_element_type=jnp.float32)
    gain_grad = jnp.sum(dround * normed, axis=0)
    dnorm = dround * gain[None, :]
    dhidden = scale * (dnorm - normed * jnp.mean(dnorm * normed, axis=1, keepdims=True))
    return (dhidden.astype(jnp.bfloat16), gain_grad, in_grad, out_grad)


def count_lists(lists, column_ids):
    tallies = jnp.zeros((lists.shape[0], column_ids.shape[1]), jnp.float32)
    for slot in range(lists.shape[1]):
        tallies = tallies + (lists[:, slot][:, None] == column_ids).astype(jnp.float32)
    return tallies


def body(counts, tile_mask, neighbours, peak_weight, gain, w_in, w_out):
    total_cells = counts.shape[0]
    own_rows = neighbours.shape[0]
    position = lax.axis_index(("grp", "peak"))
    first_row = position * own_rows
    masked = counts * jnp.repeat(tile_mask.astype(jnp.bfloat16), TILE, axis=1)
    whole_term = jnp.dot(masked, peak_weight, preferred_element_type=jnp.float32)
    hidden = lax.psum_scatter(whole_term, ("grp", "peak"), scatter_dimension=0, tiled=True)
    saved, sample_vectors = tower_forward(hidden, gain, w_in, w_out)
    codes_whole = lax.all_gather(sample_vectors, ("grp", "peak"), axis=0, tiled=True)
    affinity_scores = (
        jnp.einsum("ce,ke->ck", sample_vectors, codes_whole, preferred_element_type=jnp.float32)
        / sharpness_divisor
    )
    row_ids = lax.broadcasted_iota(jnp.int32, (own_rows, total_cells), 0) + first_row
    col_ids = lax.broadcasted_iota(jnp.int32, (own_rows, total_cells), 1)
    expo = jnp.where(row_ids == col_ids, jnp.float32(0.0), jnp.exp(affinity_scores))
    row_total = jnp.sum(expo, axis=1, keepdims=True)
    prob = expo / row_total
    neighbour_coefficients = (prob - count_lists(neighbours, col_ids) / K).astype(jnp.bfloat16)
    source_portion = jnp.dot(
        neighbour_coefficients, codes_whole, preferred_element_type=jnp.float32
    )
    target_portion = lax.psum_scatter(
        collapsed_lines(neighbour_coefficients, sample_vectors),
        ("grp", "peak"),
        scatter_dimension=0,
        tiled=True,
    )
    vector_derivative = (source_portion + target_portion) / sharpness_divisor
    dhidden, gain_part, in_part, out_part = tower_backward(
        vector_derivative, gain, w_in, w_out, saved
    )
    gain_grad, in_grad, out_grad = lax.psum((gain_part, in_part, out_part), ("grp", "peak"))
    dhidden_whole = lax.all_gather(dhidden, ("grp", "peak"), axis=0, tiled=True)
    peak_grad = collapsed_lines(masked, dhidden_whole)
    return (peak_grad, gain_grad, in_grad, out_grad)


def solution(mesh):
    placed = (
        P(None, ("grp", "peak")),
        P(None, ("grp", "peak")),
        P(("grp", "peak"), None),
        P(("grp", "peak"), None),
        P(),
        P(),
        P(),
    )
    return jax.shard_map(
        body,
        mesh=mesh,
        in_specs=placed,
        out_specs=(P(("grp", "peak"), None), P(), P(), P()),
        check_vma=False,
    )
```

profile of v0, /device:TPU:2, one launch (start us, length us, event | category | flops | bytes accessed | tf_op | source)
XLA Modules:
  0.0 2083.6 jit_solution(7782951324887230128)
XLA Ops:
  7.2 0.0 copy-start
  7.2 0.0 all-reduce.7.cloned.1.call-start
  7.2 1.0 convert_element_type.69
  8.2 0.2 copy.12
  8.4 0.0 copy-start.6
  8.4 4.5 broadcast_in_dim.6
  12.9 0.0 copy-start.1
  12.9 1.9 copy-done.1
  14.8 0.0 copy-done
  14.8 0.0 copy-done.6
  14.8 0.0 copy-start.3
  14.8 0.0 copy-start.2
  14.8 0.0 copy-start.5
  14.8 0.0 copy-start.4
  14.8 3.7 fusion.5
  18.5 0.0 all-reduce.7.cloned.1.call-update
  18.5 0.0 all-reduce.9.cloned.1.call-start
  18.6 0.0 copy-done.3
  18.6 0.4 slice_reduce_fusion.14
  19.0 263.9 %all-reduce.7.cloned.1.call-done = f32[1024,512]{1,0:T(8,128)} async-done(((f32[1024,512]{1,0:T(8,128)}), f32[1024,512]{1,0:T(8,128)}) %all-reduce.7.cloned.1.call-update) | async-done | bytes 2097168
  282.9 0.8 multiply_reduce_fusion.2
  283.8 0.0 copy-done.2
  283.8 0.0 copy-done.5
  283.8 0.9 fusion.14
  284.7 0.0 copy-done.4
  284.7 0.3 multiply_reduce_fusion.4
  285.0 0.1 fusion.33
  285.1 603.9 %all-gather = bf16[256,4,256]{2,1,0:T(4,128)(2,1)S(1)} all-gather(bf16[1,4,256]{2,1,0:T(4,128)(2,1)S(1)} %fusion.33), channel_id=1, replica_groups=mesh['grp'=16,'peak'=16] {'grp','peak'}, dimensions={0}, use_global_device_ids=true | all-gather | bytes 526336 | tf_op jit(solution)/shard_map/all_gather | solution.py:80
  889.0 0.9 reshape.34
  889.9 1.4 fusion.20
  891.3 1.4 fusion.17
  892.7 0.0 all-reduce.9.cloned.1.call-update
  892.8 0.0 all-gather.4.cloned.1.call-start
  892.8 385.1 %all-reduce.9.cloned.1.call-done = f32[1024,256]{1,0:T(8,128)} async-done(((f32[1024,256]{1,0:T(8,128)}), f32[1024,256]{1,0:T(8,128)}) %all-reduce.9.cloned.1.call-update) | async-done | bytes 1048592
  1278.0 1.4 multiply_reduce_fusion.3
  1279.4 0.2 fusion.2
  1279.6 1.1 multiply_reduce_fusion
  1280.7 1.4 fusion.12
  1282.1 0.0 all-gather.4.cloned.1.call-update
  1282.1 0.0 all-reduce.11.cloned.1.call-start
  1282.1 75.4 %psum.21 = f32[512]{0:T(512)} all-reduce(f32[512]{0:T(512)S(1)} %get-tuple-element.4), channel_id=1, replica_groups=mesh['grp'=16,'peak'=16] {'grp','peak'}, use_global_device_ids=true, to_apply=%region_8.9 | all-reduce | flops 512 | bytes 4096 | tf_op jit(solution)/shard_map/psum | solution.py:104
  1357.6 1.1 fusion.15
  1358.7 2.1 fusion.13
  1360.8 0.0 all-reduce.11.cloned.1.call-update
  1360.8 449.7 %all-gather.4.cloned.1.call-done = bf16[256,4,512]{2,1,0:T(4,128)(2,1)} async-done(((bf16[1,4,512]{2,1,0:T(4,128)(2,1)}), bf16[256,4,512]{2,1,0:T(4,128)(2,1)}) %all-gather.4.cloned.1.call-update) | async-done | bytes 1048592 | tf_op jit(solution)/shard_map/all_gather | solution.py:105
  1810.4 1.3 reshape.36
  1811.8 8.1 fusion.4
  1819.9 253.0 %all-reduce.11.cloned.1.call-done = (f32[512,512]{1,0:T(8,128)}, f32[512,256]{1,0:T(8,128)}) async-done(((f32[512,512]{1,0:T(8,128)}, f32[512,256]{1,0:T(8,128)}), (f32[512,512]{1,0:T(8,128)}, f32[512,256]{1,0:T(8,128)})) %all-reduce.11.cloned.1.call-update) | async-done | bytes 1572880 | tf_op jit(solution)/shard_map/psum | solution.py:104
  2072.9 2.3 copy.21
  2075.2 1.9 copy.22
  (4 shorter events, 0.0 us)
Async XLA Ops:
  7.2 7.6 copy-start
  7.2 275.7 %all-reduce.7.cloned.1.call-start = ((), (), s32[]{:S(2)}) async-start(), calls=%async_computation.1 | async-start | bytes 4194304
  8.4 6.4 copy-start.6
  12.9 1.9 copy-start.1
  14.8 3.8 copy-start.3
  14.8 269.0 %copy-start.2 = (bf16[512,512]{1,0:T(8,128)(2,1)S(1)}, bf16[512,512]{1,0:T(8,128)(2,1)}, u32[]{:S(2)}) copy-start(bf16[512,512]{1,0:T(8,128)(2,1)} %param.12) | copy-start | bytes 1572868
  14.8 269.0 %copy-start.5 = (f32[512]{0:T(512)S(1)}, f32[512]{0:T(512)}, u32[]{:S(2)}) copy-start(f32[512]{0:T(512)} %param.11) | copy-start | bytes 6148
  14.8 269.9 %copy-start.4 = (bf16[512,256]{1,0:T(8,128)(2,1)S(1)}, bf16[512,256]{1,0:T(8,128)(2,1)}, u32[]{:S(2)}) copy-start(bf16[512,256]{1,0:T(8,128)(2,1)} %param.13) | copy-start | bytes 786436
  18.5 1259.4 %all-reduce.9.cloned.1.call-start = ((), (), s32[]{:S(2)}) async-start(), calls=%async_computation.2 | async-start | bytes 2097152
  892.8 917.7 %all-gather.4.cloned.1.call-start = ((), (), s32[]{:S(2)}) async-start(), calls=%async_computation | async-start | bytes 1052672 | tf_op jit(solution)/shard_map/all_gather | solution.py:105
  1282.1 790.9 %all-reduce.11.cloned.1.call-start = ((), (), s32[]{:S(2)}) async-start(), calls=%async_computation.3 | async-start | bytes 3145728 | tf_op jit(solution)/shard_map/psum | solution.py:104
Sparse Core Ops, SparseCore 0:
  18.6 264.2 all-reduce.6
  892.9 385.0 all-reduce.8
  1282.2 528.1 all-gather.3
  1817.2 255.7 all-reduce.10
where the time goes:
time: 2080 us
  waiting for transfers between devices  1350 us (65%)
  blocking collectives  679 us (33%)
  matrix products  21.7 us (1%)
    unnamed x6, waiting for transfers between devices  649 us
    all_gather x1, blocking collectives, body(): lax.all_gather(sample_vectors, ('grp', 'peak'), axis=0, tiled=True)  604 us
    all_gather x1, waiting for transfers between devices, body(): dhidden_whole = lax.all_gather(dhidden, ('grp', 'peak'), axis=0, tiled=True)  450 us
    psum x1, waiting for transfers between devices, body(): lax.psum((gain_part, in_part, out_part), ('grp', 'peak'))  253 us
    psum x1, blocking collectives, body(): lax.psum((gain_part, in_part, out_part), ('grp', 'peak'))  75.4 us
  transfers between devices with their start and end apart: 4, of which 4 were waited for; matrix products, arithmetic and copies ran while one was open for 1% of the time, Pallas kernels for 0%

commit v1 on v0

--- a/solution.py
+++ b/solution.py
@@ -9,6 +9,11 @@
 eps_norm = 1e-06
 gelu_coef = 0.7978845608
 cubic_coef = 0.044715
+
+
+def gather_over(value, name, d):
+    repeated = jnp.stack([value] * lax.axis_size(name))
+    return jnp.concatenate(lax.all_to_all(repeated, name, 0, 0), axis=d)
 
 
 def gelu_tanh(values):
@@ -77,7 +82,7 @@
     whole_term = jnp.dot(masked, peak_weight, preferred_element_type=jnp.float32)
     hidden = lax.psum_scatter(whole_term, ("grp", "peak"), scatter_dimension=0, tiled=True)
     saved, sample_vectors = tower_forward(hidden, gain, w_in, w_out)
-    codes_whole = lax.all_gather(sample_vectors, ("grp", "peak"), axis=0, tiled=True)
+    codes_whole = gather_over(sample_vectors, ("grp", "peak"), 0)
     affinity_scores = (
         jnp.einsum("ce,ke->ck", sample_vectors, codes_whole, preferred_element_type=jnp.float32)
         / sharpness_divisor

time: 2080 us -> 1380 us (0.66)
  blocking collectives: 679 us -> 75.4 us
  waiting for transfers between devices: 1350 us -> 1240 us
    all_gather x1 -> x0, blocking collectives: 604 us -> none  [body(): lax.all_gather(sample_vectors, ('grp', 'peak'), axis=0, tiled=True)]
    unnamed x6, waiting for transfers between devices: 649 us -> 515 us
  transfers between devices with their start and end apart: 4 -> 5, of which waited for: 4 -> 5; matrix products, arithmetic and copies ran while one was open for 1% -> 1% of each run, Pallas kernels for 0% -> 0%
where the time goes in v1:
time: 1380 us
  waiting for transfers between devices  1240 us (90%)
  blocking collectives  75.4 us (5%)
  matrix products  21.7 us (2%)
  local copies, waits for them, and re-layouts  14.3 us (1%)
  between operations  13.9 us (1%)
    unnamed x6, waiting for transfers between devices  515 us
    all_gather x1, waiting for transfers between devices, body(): dhidden_whole = lax.all_gather(dhidden, ('grp', 'peak'), axis=0, tiled=True)  450 us
    psum x1, waiting for transfers between devices, body(): lax.psum((gain_part, in_part, out_part), ('grp', 'peak'))  253 us
    psum x1, blocking collectives, body(): lax.psum((gain_part, in_part, out_part), ('grp', 'peak'))  75.4 us
  transfers between devices with their start and end apart: 5, of which 5 were waited for; matrix products, arithmetic and copies ran while one was open for 1% of the time, Pallas kernels for 0%

profile of v1, /device:TPU:2, one launch (start us, length us, event | category | flops | bytes accessed | tf_op | source)
XLA Modules:
  0.0 1375.8 jit_solution(15516730377406292002)
XLA Ops:
  7.2 0.0 copy-start
  7.2 0.0 all-reduce.7.cloned.1.call-start
  7.2 1.0 convert_element_type.69
  8.2 0.2 copy.12
  8.4 0.0 copy-start.6
  8.4 4.5 broadcast_in_dim.6
  12.9 0.0 copy-start.1
  12.9 1.9 copy-done.1
  14.8 0.0 copy-done
  14.8 0.0 copy-done.6
  14.8 0.0 copy-start.2
  14.8 0.0 copy-start.5
  14.8 0.0 copy-start.4
  14.8 3.7 fusion.5
  18.5 0.0 copy-start.3
  18.5 0.0 all-reduce.7.cloned.1.call-update
  18.5 264.4 %all-reduce.7.cloned.1.call-done = f32[1024,512]{1,0:T(8,128)} async-done(((f32[1024,512]{1,0:T(8,128)}), f32[1024,512]{1,0:T(8,128)}) %all-reduce.7.cloned.1.call-update) | async-done | bytes 2097168
  282.9 0.8 multiply_reduce_fusion.2
  283.8 0.0 copy-done.2
  283.8 0.0 copy-done.5
  283.8 0.9 fusion.14
  284.7 0.0 copy-done.4
  284.7 0.3 multiply_reduce_fusion.4
  285.0 0.1 multiply_convert_fusion.4
  285.1 0.9 stack.2
  286.0 10.4 all-to-all-start
  296.4 0.0 all-reduce.9.cloned.1.call-start
  296.5 0.0 copy-done.3
  296.5 0.4 slice_reduce_fusion.14
  296.9 19.3 %all-to-all-done = bf16[256,4,256]{2,1,0:T(4,128)(2,1)S(1)} async-done(((bf16[256,4,256]{2,1,0:T(4,128)(2,1)}), bf16[256,4,256]{2,1,0:T(4,128)(2,1)S(1)}, u32[]{:S(2)}, u32[]{:S(2)}) %all-to-all-start) | async-done | bytes 524320 | tf_op jit(solution)/shard_map/all_to_all | solution.py:16
  316.2 0.9 reshape.38
  317.2 1.4 fusion.20
  318.6 1.4 fusion.17
  320.0 0.0 all-reduce.9.cloned.1.call-update
  320.0 0.0 all-gather.3.cloned.1.call-start
  320.1 250.2 %all-reduce.9.cloned.1.call-done = f32[1024,256]{1,0:T(8,128)} async-done(((f32[1024,256]{1,0:T(8,128)}), f32[1024,256]{1,0:T(8,128)}) %all-reduce.9.cloned.1.call-update) | async-done | bytes 1048592
  570.3 1.4 multiply_reduce_fusion.3
  571.7 0.2 fusion.2
  571.9 1.1 multiply_reduce_fusion
  573.0 1.4 fusion.12
  574.4 0.0 all-gather.3.cloned.1.call-update
  574.4 0.0 all-reduce.11.cloned.1.call-start
  574.5 75.4 %psum.21 = f32[512]{0:T(512)} all-reduce(f32[512]{0:T(512)S(1)} %get-tuple-element.4), channel_id=1, replica_groups=mesh['grp'=16,'peak'=16] {'grp','peak'}, use_global_device_ids=true, to_apply=%region_8.9 | all-reduce | flops 512 | bytes 4096 | tf_op jit(solution)/shard_map/psum | solution.py:109
  649.9 1.1 fusion.15
  651.0 2.1 fusion.13
  653.1 0.0 all-reduce.11.cloned.1.call-update
  653.1 449.7 %all-gather.3.cloned.1.call-done = bf16[256,4,512]{2,1,0:T(4,128)(2,1)} async-done(((bf16[1,4,512]{2,1,0:T(4,128)(2,1)}), bf16[256,4,512]{2,1,0:T(4,128)(2,1)}) %all-gather.3.cloned.1.call-update) | async-done | bytes 1048592 | tf_op jit(solution)/shard_map/all_gather | solution.py:110
  1102.8 1.3 reshape.40
  1104.1 8.1 fusion.4
  1112.2 252.9 %all-reduce.11.cloned.1.call-done = (f32[512,512]{1,0:T(8,128)}, f32[512,256]{1,0:T(8,128)}) async-done(((f32[512,512]{1,0:T(8,128)}, f32[512,256]{1,0:T(8,128)}), (f32[512,512]{1,0:T(8,128)}, f32[512,256]{1,0:T(8,128)})) %all-reduce.11.cloned.1.call-update) | async-done | bytes 1572880 | tf_op jit(solution)/shard_map/psum | solution.py:109
  1365.1 2.3 copy.21
  1367.4 1.9 copy.22
  (4 shorter events, 0.0 us)
Async XLA Ops:
  7.2 7.6 copy-start
  7.2 275.8 %all-reduce.7.cloned.1.call-start = ((), (), s32[]{:S(2)}) async-start(), calls=%async_computation.2 | async-start | bytes 4194304
  8.4 6.4 copy-start.6
  12.9 1.9 copy-start.1
  14.8 269.0 %copy-start.2 = (bf16[512,512]{1,0:T(8,128)(2,1)S(1)}, bf16[512,512]{1,0:T(8,128)(2,1)}, u32[]{:S(2)}) copy-start(bf16[512,512]{1,0:T(8,128)(2,1)} %param.12) | copy-start | bytes 1572868
  14.8 269.0 %copy-start.5 = (f32[512]{0:T(512)S(1)}, f32[512]{0:T(512)}, u32[]{:S(2)}) copy-start(f32[512]{0:T(512)} %param.11) | copy-start | bytes 6148
  14.8 269.9 %copy-start.4 = (bf16[512,256]{1,0:T(8,128)(2,1)S(1)}, bf16[512,256]{1,0:T(8,128)(2,1)}, u32[]{:S(2)}) copy-start(bf16[512,256]{1,0:T(8,128)(2,1)} %param.13) | copy-start | bytes 786436
  18.5 278.0 %copy-start.3 = (s32[4,15]{1,0:T(4,128)S(1)}, s32[4,15]{1,0:T(4,128)}, u32[]{:S(2)}) copy-start(s32[4,15]{1,0:T(4,128)} %param.9) | copy-start | bytes 724
  286.0 30.2 %all-to-all-start = ((bf16[256,4,256]{2,1,0:T(4,128)(2,1)}), bf16[256,4,256]{2,1,0:T(4,128)(2,1)S(1)}, u32[]{:S(2)}, u32[]{:S(2)}) async-start(bf16[256,4,256]{2,1,0:T(4,128)(2,1)} %stack.2), calls=%async_computation | async-start | bytes 1048576 | tf_op jit(solution)/shard_map/all_to_all | solution.py:16
  296.4 273.9 %all-reduce.9.cloned.1.call-start = ((), (), s32[]{:S(2)}) async-start(), calls=%async_computation.3 | async-start | bytes 2097152
  320.0 782.8 %all-gather.3.cloned.1.call-start = ((), (), s32[]{:S(2)}) async-start(), calls=%async_computation.1 | async-start | bytes 1052672 | tf_op jit(solution)/shard_map/all_gather | solution.py:110
  574.4 790.7 %all-reduce.11.cloned.1.call-start = ((), (), s32[]{:S(2)}) async-start(), calls=%async_computation.4 | async-start | bytes 3145728 | tf_op jit(solution)/shard_map/psum | solution.py:109
Sparse Core Ops, SparseCore 0:
  18.6 264.2 all-reduce.6
  320.1 250.1 all-reduce.8
  574.5 528.1 all-gather.2
  1109.5 255.5 all-reduce.10
